TPU v7x, 512 devices: a whole 4x4x16 slice. The times are simulated.
512 devices in a mesh: tile: 32 (over y, x, core), fsdp: 16 (over z).
Axes of the slice: x: 4, y: 4, z: 16, core: 2. Of those that a mesh axis runs over, the one named last changes fastest.
Arguments:
- images: bfloat16 [16, 32, 8, 128, 320], P('fsdp', 'tile'), may hold values from -80 to 80
- tile_rows: int32 [16, 32], P('fsdp', 'tile'), may hold values from 1 to 8, 160 in all within a row
- cotangent: bfloat16 [16, 32, 8, 128, 320], P('fsdp', 'tile'), may hold values from -6 to 6
- master_weight: float32 [2880, 320], P('fsdp'), may hold values from -0.109375 to 0.109375
- norm_gain: float32 [320], replicated, may hold values from 0.5 to 1.5
- norm_bias: float32 [320], replicated, may hold values from -3 to 3
- first_moment: float32 [2880, 320], P('fsdp'), may hold values from -6 to 6
- second_moment: float32 [2880, 320], P('fsdp'), may hold values from 0.5 to 4
Outputs:
- activation: bfloat16 [16, 32, 8, 128, 320], P('fsdp', 'tile')
- image_grad: bfloat16 [16, 32, 8, 128, 320], P('fsdp', 'tile')
- weight_grad: float32 [2880, 320], P('fsdp')
- new_weight: float32 [2880, 320], P('fsdp')
- new_first: float32 [2880, 320], P('fsdp')
- new_second: float32 [2880, 320], P('fsdp')
- gain_grad: float32 [320], replicated
- bias_grad: float32 [320], replicated
Inputs may be any that keep to these rules, and one draw needn't show every extreme that they name: `tile_rows`: in each frame the 32 counts sum to 160 and the largest is exactly 8.
All inputs are finite; a program needn't handle non-finite values. No bound on the sum of `tile_rows` on one device may be relied on, other than what follows from the above.
Results may differ from a plain program's by a relative error of at most 0.027.
Values may be sent and summed in bfloat16 or wider, within the bound.
No kernel may reach another device: no remote copies, remote signals or barrier semaphores. Data moves between devices by JAX's collectives and lax.ppermute only.
A program may use at most 64 MiB of HBM per device.

v0:
```python
import jax
import jax.numpy as jnp
from jax import lax
from jax.sharding import PartitionSpec as P

GROUPS = 32
ROWS_MEAN = 5


def extended(cells, sides, width):
    for axis, dim in sides:
        count = lax.axis_size(axis)
        ends = count - 1
        head = lax.slice_in_dim(cells, 0, width, axis=dim)
        tail = lax.slice_in_dim(cells, cells.shape[dim] - width, cells.shape[dim], axis=dim)
        cells = jnp.concatenate(
            [
                lax.ppermute(tail, axis, [(i, (i + 1) % count) for i in range(ends)]),
                cells,
                lax.ppermute(head, axis, [((i + 1) % count, i) for i in range(ends)]),
            ],
            axis=dim,
        )
    return cells


def edge_pair(source, live_count):
    first_row = source[0:1]
    last_row = lax.dynamic_slice_in_dim(source, live_count - 1, 1, 0)
    return jnp.concatenate([first_row, last_row], axis=0)


def framed(source, beside_all, live_count):
    slot_count = source.shape[0]
    zero_row = jnp.zeros_like(source[0:1])
    stacked = jnp.concatenate([beside_all[0:1], source, zero_row], axis=0)
    marker = (jnp.arange(slot_count + 2) == live_count + 1)[:, None, None]
    stacked = jnp.where(marker, beside_all[3:4], stacked)
    return jnp.pad(stacked, ((0, 0), (1, 1), (0, 0)))


def patches_of(padded, slot_count, cell_cols):
    pieces = [
        padded[row_step : row_step + slot_count, col_step : col_step + cell_cols, :]
        for row_step in range(3)
        for col_step in range(3)
    ]
    return jnp.concatenate(pieces, axis=-1).reshape(slot_count * cell_cols, -1)


def local(
    images, tile_rows, cotangent, master_weight, norm_gain, norm_bias, first_moment, second_moment
):
    slot_count, cell_cols, channels = (images.shape[2], images.shape[3], images.shape[4])
    per_group = channels // GROUPS
    tile_count = lax.axis_size("tile")
    shards = lax.axis_size("fsdp")
    population = jnp.float32(ROWS_MEAN * tile_count * cell_cols * per_group)
    live_count = tile_rows[0, 0]
    live_rows = jnp.arange(slot_count) < live_count
    cell_mask = jnp.repeat(live_rows, cell_cols).astype(jnp.float32)[:, None]

    def grouped(values):
        return jnp.sum(values.reshape(-1, GROUPS, per_group), axis=(0, 2))

    def spread(stat):
        return jnp.repeat(stat, per_group)

    source = jnp.where(live_rows[:, None, None], images[0, 0], jnp.zeros((), jnp.bfloat16))
    beside_all = extended(edge_pair(source, live_count), (("tile", 0),), 1)
    columns = patches_of(framed(source, beside_all, live_count), slot_count, cell_cols)
    gathered = lax.all_gather(master_weight.astype(jnp.bfloat16), "fsdp", axis=0, tiled=True)
    mixed = jnp.dot(columns, gathered, preferred_element_type=jnp.float32)
    group_mean = lax.psum(grouped(mixed * cell_mask), "tile") / population
    centered = (mixed - spread(group_mean)) * cell_mask
    variance = lax.psum(grouped(centered * centered), "tile") / population
    inverse = lax.rsqrt(variance + 1e-05)
    normed = (mixed - spread(group_mean)) * spread(inverse)
    shifted = normed * norm_gain + norm_bias
    gate_value = jax.nn.sigmoid(shifted)
    activation = (shifted * gate_value * cell_mask).astype(jnp.bfloat16).reshape(images.shape)
    upstream = cotangent[0, 0].reshape(-1, channels).astype(jnp.float32) * cell_mask
    dshift = upstream * gate_value * (1.0 + shifted * (1.0 - gate_value))
    scaled = dshift * norm_gain
    delta_sum, cross_sum = lax.psum((grouped(scaled), grouped(scaled * normed)), "tile")
    gain_total, bias_total = lax.psum(
        (jnp.sum(dshift * normed, axis=0), jnp.sum(dshift, axis=0)), ("tile", "fsdp")
    )
    norm_scale = jnp.float32(shards * ROWS_MEAN * tile_count * cell_cols) ** (-0.5)
    pre_grad = spread(inverse) * (
        scaled - spread(delta_sum / population) - normed * spread(cross_sum / population)
    )
    pre_grad = (pre_grad * cell_mask).astype(jnp.bfloat16)
    grad_field = pre_grad.reshape(slot_count, cell_cols, channels)
    grad_around = extended(edge_pair(grad_field, live_count), (("tile", 0),), 1)
    grad_columns = patches_of(framed(grad_field, grad_around, live_count), slot_count, cell_cols)
    flipped = (
        gathered.reshape(9, channels, channels)[::-1]
        .transpose(0, 2, 1)
        .reshape(9 * channels, channels)
    )
    image_grad = (
        (jnp.dot(grad_columns, flipped, preferred_element_type=jnp.float32) * cell_mask)
        .astype(jnp.bfloat16)
        .reshape(images.shape)
    )
    full_grad = lax.psum(
        lax.dot_general(
            columns, pre_grad, (((0,), (0,)), ((), ())), preferred_element_type=jnp.float32
        ).astype(jnp.bfloat16),
        "tile",
    )
    grad_shard = lax.psum_scatter(full_grad, "fsdp", scatter_dimension=0, tiled=True).astype(
        jnp.float32
    )
    weight_grad = grad_shard * norm_scale
    new_first = 0.9 * first_moment + 0.1 * weight_grad
    new_second = 0.999 * second_moment + 0.001 * weight_grad * weight_grad
    first_fix = new_first / (1.0 - 0.9**10)
    second_fix = new_second / (1.0 - 0.999**10)
    new_weight = master_weight - 0.01 * first_fix / (jnp.sqrt(second_fix) + 1e-08)
    return (
        activation,
        image_grad,
        weight_grad,
        new_weight,
        new_first,
        new_second,
        gain_total * norm_scale,
        bias_total * norm_scale,
    )


def solution(mesh):
    placed = (
        P("fsdp", "tile", None, None, None),
        P("fsdp", "tile"),
        P("fsdp", "tile", None, None, None),
        P("fsdp", None),
        P(),
        P(),
        P("fsdp", None),
        P("fsdp", None),
    )
    return jax.shard_map(
        local,
        mesh=mesh,
        in_specs=placed,
        out_specs=(
            P("fsdp", "tile", None, None, None),
            P("fsdp", "tile", None, None, None),
            P("fsdp", None),
            P("fsdp", None),
            P("fsdp", None),
            P("fsdp", None),
            P(),
            P(),
        ),
        check_vma=False,
    )
```

profile of v0, /device:TPU:1, one launch (start us, length us, event | category | flops | bytes accessed | tf_op | source)
XLA Modules:
  0.0 609.0 jit_solution(12582963821743056391)
XLA Ops:
  7.2 1.7 convert_bitcast_fusion
  9.7 1.2 bitcast_select_fusion
  10.9 8.8 %collective-permute-start = (bf16[1,128,320]{1,2,0:T(8,128)(2,1)S(1)}, bf16[1,128,320]{1,2,0:T(8,128)(2,1)S(1)}, u32[]{:S(2)}, u32[]{:S(2)}) collective-permute-start(bf16[1,128,320]{1,2,0:T(8,128)(2,1)S(1)} %get-tuple-element.46), channel_id=1, source_target_pairs={{16,0},{32,16},{48,32},{64,48},{80,64},{96,80},{112,96},{128,112},... | collective-permute-start | bytes 245768 | tf_op jit(solution)/shard_map/ppermute | solution.py:20
  19.7 1.9 collective-permute-start.1
  21.6 1.5 copy.30
  23.2 1.3 dynamic-slice.4
  27.5 1.1 fusion.6
  28.6 1.1 fusion.7
  34.9 8.4 %copy.29 = bf16[8,128,2880]{2,1,0:T(8,128)(2,1)} copy(bf16[8,128,2880]{1,2,0:T(8,128)(2,1)} %fusion.10) | data formatting | bytes 11796480 | tf_op jit(solution)/shard_map/concatenate | solution.py:48
  43.4 37.7 %all-gather.3.cloned.1.call-done = bf16[16,180,320]{2,1,0:T(8,128)(2,1)} async-done(((bf16[1,180,320]{2,1,0:T(8,128)(2,1)}), bf16[16,180,320]{2,1,0:T(8,128)(2,1)}) %all-gather.3.cloned.1.call-update) | async-done | bytes 1843216 | tf_op jit(solution)/shard_map/all_gather | solution.py:72
  81.1 2.8 reshape.78
  83.8 5.1 multiply_reduce_fusion.3
  89.1 71.5 %psum.49 = f32[32]{0:T(128)S(1)} all-reduce(f32[32]{0:T(128)S(1)} %reduce_sum.67), channel_id=1, replica_groups=mesh['tile'=32,'fsdp'=16] {'tile'}, use_global_device_ids=true, to_apply=%region_2.3 | all-reduce | flops 32 | bytes 256 | tf_op jit(solution)/shard_map/psum | solution.py:74
  161.4 62.7 %psum.50 = f32[32]{0:T(128)S(1)} all-reduce(f32[32]{0:T(128)S(1)} %reduce_sum.73), channel_id=1, replica_groups=mesh['tile'=32,'fsdp'=16] {'tile'}, use_global_device_ids=true, to_apply=%region_5.6 | all-reduce | flops 32 | bytes 256 | tf_op jit(solution)/shard_map/psum | solution.py:76
  224.3 3.5 multiply_reduce_fusion
  228.2 62.9 %all-reduce.5 = (f32[32]{0:T(128)S(1)}, f32[32]{0:T(128)S(1)}) all-reduce(f32[32]{0:T(128)S(1)} %reduce_sum.93, f32[32]{0:T(128)S(1)} %reduce_sum.90), channel_id=1, replica_groups=mesh['tile'=32,'fsdp'=16] {'tile'}, use_global_device_ids=true, to_apply=%region_11.12 | all-reduce | flops 64 | bytes 512 | tf_op jit(solution)/shard_map/psum | solution.py:85
  292.3 7.4 %convolution_convert_fusion = bf16[2880,320]{1,0:T(8,128)(2,1)} fusion(bf16[1024,2880]{1,0:T(8,128)(2,1)} %bitcast.60, bf16[1024,320]{0,1:T(8,128)(2,1)S(1)} %multiply_convert_fusion), kind=kOutput, calls=%fused_computation | convolution fusion | flops 1888358400 | bytes 8396800 | tf_op jit(solution)/shard_map/dot_general | solution.py:108
  300.5 33.6 %fusion = bf16[192,320]{1,0:T(8,128)(2,1)S(1)} fusion(bf16[2880,320]{1,0:T(8,128)(2,1)} %convolution_convert_fusion), kind=kCustom, calls=%all-reduce-scatter | all-reduce-scatter fusion | flops 983041 | bytes 1968128
  334.1 2.7 collective-permute-start.4
  337.5 5.1 collective-permute-start.3
  342.6 5.2 collective-permute-start.2
  347.8 100.6 %all-reduce.4 = (f32[320]{0:T(512)S(1)}, f32[320]{0:T(512)S(1)}) all-reduce(f32[320]{0:T(512)S(1)} %get-tuple-element.32, f32[320]{0:T(512)S(1)} %get-tuple-element.35), channel_id=1, replica_groups=mesh['tile'=32,'fsdp'=16] {'tile','fsdp'}, use_global_device_ids=true, to_apply=%region_15.16 | all-reduce | flops 640 | bytes 5120 | tf_op jit(solution)/shard_map/psum | solution.py:86
  449.0 2.2 reshape.73
  451.2 1.8 reverse_bitcast_fusion
  453.1 2.5 copy.34
  455.6 1.2 copy.38
  460.0 1.1 fusion.12
  461.2 1.1 fusion.13
  467.5 8.6 %copy.33 = bf16[8,128,2880]{2,1,0:T(8,128)(2,1)} copy(bf16[8,128,2880]{1,2,0:T(8,128)(2,1)} %fusion.16) | data formatting | bytes 11796480 | tf_op jit(solution)/shard_map/concatenate | solution.py:48
  477.7 4.9 fusion.4
  483.8 116.3 %all-reduce.8.cloned.1.call-done = bf16[180,320]{1,0:T(8,128)(2,1)} async-done(((bf16[180,320]{1,0:T(8,128)(2,1)}), bf16[180,320]{1,0:T(8,128)(2,1)}) %all-reduce.8.cloned.1.call-update) | async-done | bytes 115216 | tf_op jit(solution)/shard_map/psum | solution.py:107
  600.1 2.0 divide_subtract_fusion
  (78 shorter events, 23.8 us)
Async XLA Ops:
  7.2 14.4 %copy-start.3 = (bf16[1,1,8,128,320]{3,4,2,1,0:T(8,128)(2,1)S(1)}, bf16[1,1,8,128,320]{3,4,2,1,0:T(8,128)(2,1)}, u32[]{:S(2)}) copy-start(bf16[1,1,8,128,320]{3,4,2,1,0:T(8,128)(2,1)} %param.10) | copy-start | bytes 1966084
  7.2 73.9 %all-gather.3.cloned.1.call-start = ((), (), s32[]{:S(2)}) async-start(), calls=%async_computation.1 | async-start | bytes 2402304 | tf_op jit(solution)/shard_map/all_gather | solution.py:72
  8.9 591.2 %all-reduce.8.cloned.1.call-start = ((), (), s32[]{:S(2)}) async-start(), calls=%async_computation | async-start | bytes 282624 | tf_op jit(solution)/shard_map/psum | solution.py:107
  10.9 14.3 %collective-permute-start = (bf16[1,128,320]{1,2,0:T(8,128)(2,1)S(1)}, bf16[1,128,320]{1,2,0:T(8,128)(2,1)S(1)}, u32[]{:S(2)}, u32[]{:S(2)}) collective-permute-start(bf16[1,128,320]{1,2,0:T(8,128)(2,1)S(1)} %get-tuple-element.46), channel_id=1, source_target_pairs={{16,0},{32,16},{48,32},{64,48},{80,64},{96,80},{112,96},{128,112},... | collective-permute-start | bytes 245768 | tf_op jit(solution)/shard_map/ppermute | solution.py:20
  19.7 5.5 collective-permute-start.1
  83.8 140.5 %copy-start.6 = (f32[320]{0:T(512)S(1)}, f32[320]{0:T(512)}, u32[]{:S(2)}) copy-start(f32[320]{0:T(512)} %param.12) | copy-start | bytes 3844
  83.8 140.5 %copy-start.7 = (f32[320]{0:T(512)S(1)}, f32[320]{0:T(512)}, u32[]{:S(2)}) copy-start(f32[320]{0:T(512)} %param.13) | copy-start | bytes 3844
  299.8 149.2 %copy-start = (bf16[16,180,320]{2,1,0:T(8,128)(2,1)S(1)}, bf16[16,180,320]{2,1,0:T(8,128)(2,1)}, u32[]{:S(2)}) copy-start(bf16[16,180,320]{2,1,0:T(8,128)(2,1)} %all-gather.3.cloned.1.call-done) | copy-start | bytes 5529604
  334.1 141.9 %collective-permute-start.4 = (bf16[180,320]{1,0:T(8,128)(2,1)S(1)}, bf16[180,320]{1,0:T(8,128)(2,1)S(1)}, u32[]{:S(2)}, u32[]{:S(2)}) collective-permute-start(bf16[180,320]{1,0:T(8,128)(2,1)S(1)} %slice.98), channel_id=1, source_target_pairs={{0,1},{1,2},{2,3},{3,4},{4,5},{5,6},{6,7},{7,8},{8,9},{9,10},{10,1... | collective-permute-start | bytes 345608
  337.5 120.2 %collective-permute-start.3 = (bf16[1,128,320]{1,2,0:T(8,128)(2,1)}, bf16[1,128,320]{1,2,0:T(8,128)(2,1)S(1)}, u32[]{:S(2)}, u32[]{:S(2)}) collective-permute-start(bf16[1,128,320]{1,2,0:T(8,128)(2,1)} %constant_dynamic-slice_fusion.1), channel_id=1, source_target_pairs={{0,16},{16,32},{32,48},{48,64},{64,80},{80,96},{96,112},{112,128},... | collective-permute-start | bytes 245768 | tf_op jit(solution)/shard_map/ppermute | solution.py:18
  342.6 115.2 %collective-permute-start.2 = (bf16[1,128,320]{1,2,0:T(8,128)(2,1)}, bf16[1,128,320]{1,2,0:T(8,128)(2,1)S(1)}, u32[]{:S(2)}, u32[]{:S(2)}) collective-permute-start(bf16[1,128,320]{1,2,0:T(8,128)(2,1)} %slice_bitcast_fusion), channel_id=1, source_target_pairs={{16,0},{32,16},{48,32},{64,48},{80,64},{96,80},{112,96},{128,112},... | collective-permute-start | bytes 245768 | tf_op jit(solution)/shard_map/ppermute | solution.py:20
  467.5 10.2 %copy-start.1 = (bf16[9,320,320]{2,1,0:T(8,128)(2,1)S(1)}, bf16[9,320,320]{2,1,0:T(8,128)(2,1)}, u32[]{:S(2)}) copy-start(bf16[9,320,320]{2,1,0:T(8,128)(2,1)} %copy.34) | copy-start | bytes 5529604
  482.6 117.5 %copy-start.2 = (f32[180,320]{1,0:T(8,128)S(1)}, f32[180,320]{1,0:T(8,128)}, u32[]{:S(2)}) copy-start(f32[180,320]{1,0:T(8,128)} %param.11) | copy-start | bytes 691204
  482.7 117.4 %copy-start.4 = (f32[180,320]{1,0:T(8,128)S(1)}, f32[180,320]{1,0:T(8,128)}, u32[]{:S(2)}) copy-start(f32[180,320]{1,0:T(8,128)} %param.14) | copy-start | bytes 691204
  482.7 117.4 %copy-start.5 = (f32[180,320]{1,0:T(8,128)S(1)}, f32[180,320]{1,0:T(8,128)}, u32[]{:S(2)}) copy-start(f32[180,320]{1,0:T(8,128)} %param.15) | copy-start | bytes 691204
Sparse Core Ops, SparseCore 0:
  10.7 70.3 all-gather.2
  477.8 122.2 all-reduce.7
where the time goes:
time: 610 us; the launch traced here: 609 us
  blocking collectives  331 us (54%)
  waiting for transfers between devices  154 us (25%)
  local copies, waits for them, and re-layouts  55.7 us (9%)
  starting transfers between devices  23.8 us (4%)
  matrix products  17.4 us (3%)
  between operations  15.7 us (3%)
  other arithmetic  11.1 us (2%)
    psum x1, waiting for transfers between devices, local(): lax.psum(lax.dot_general(columns, pre_grad, (((0,), (0,)), ((), ())), pre...  116 us
    psum x1, blocking collectives, local(): lax.psum((jnp.sum(dshift * normed, axis=0), jnp.sum(dshift, axis=0)), ('t...  101 us
    psum x1, blocking collectives, local(): group_mean = lax.psum(grouped(mixed * cell_mask), 'tile') / population  71.5 us
    psum x1, blocking collectives, local(): lax.psum((grouped(scaled), grouped(scaled * normed)), 'tile')  62.9 us
    psum x1, blocking collectives, local(): variance = lax.psum(grouped(centered * centered), 'tile') / population  62.7 us
    all_gather x1, waiting for transfers between devices, local(): lax.all_gather(master_weight.astype(jnp.bfloat16), 'fsdp', axis=0, tiled=...  37.7 us
    unnamed x1, blocking collectives  33.6 us
    unnamed x41, local copies, waits for them, and re-layouts  25.8 us
  transfers between devices with their start and end apart: 7, of which 2 were waited for; matrix products, arithmetic and copies ran while one was open for 9% of the time, Pallas kernels for 0%

commit v1 on v0

--- a/solution.py
+++ b/solution.py
@@ -84,7 +84,7 @@
     scaled = dshift * norm_gain
     delta_sum, cross_sum = lax.psum((grouped(scaled), grouped(scaled * normed)), "tile")
     gain_total, bias_total = lax.psum(
-        (jnp.sum(dshift * normed, axis=0), jnp.sum(dshift, axis=0)), ("tile", "fsdp")
+        lax.psum((jnp.sum(dshift * normed, axis=0), jnp.sum(dshift, axis=0)), "tile"), "fsdp"
     )
     norm_scale = jnp.float32(shards * ROWS_MEAN * tile_count * cell_cols) ** (-0.5)
     pre_grad = spread(inverse) * (

time: 610 us -> 540 us (0.89)
  blocking collectives: 331 us -> 254 us
  waiting for transfers between devices: 154 us -> 162 us
    psum x1, blocking collectives: 101 us -> 22.5 us  [local(): lax.psum(lax.psum((jnp.sum(dshift * normed, axis=0), jnp.sum(dshift, axis...]
    psum x1, waiting for transfers between devices: 116 us -> 124 us  [local(): lax.psum(lax.dot_general(columns, pre_grad, (((0,), (0,)), ((), ())), pre...]
  transfers between devices with their start and end apart: 7 -> 7, of which waited for: 2 -> 2; matrix products, arithmetic and copies ran while one was open for 9% -> 10% of each run, Pallas kernels for 0% -> 0%
where the time goes in v1:
time: 540 us; the launch traced here: 539 us
  blocking collectives  254 us (47%)
  waiting for transfers between devices  162 us (30%)
  local copies, waits for them, and re-layouts  55.7 us (10%)
  starting transfers between devices  23.8 us (4%)
  matrix products  17.4 us (3%)
  between operations  15.7 us (3%)
  other arithmetic  11.1 us (2%)
    psum x1, waiting for transfers between devices, local(): lax.psum(lax.dot_general(columns, pre_grad, (((0,), (0,)), ((), ())), pre...  124 us
    psum x1, blocking collectives, local(): group_mean = lax.psum(grouped(mixed * cell_mask), 'tile') / population  71.5 us
    psum x1, blocking collectives, local(): lax.psum((grouped(scaled), grouped(scaled * normed)), 'tile')  63.8 us
    psum x1, blocking collectives, local(): variance = lax.psum(grouped(centered * centered), 'tile') / population  62.7 us
    all_gather x1, waiting for transfers between devices, local(): lax.all_gather(master_weight.astype(jnp.bfloat16), 'fsdp', axis=0, tiled=...  37.7 us
    unnamed x1, blocking collectives  33.5 us
    unnamed x41, local copies, waits for them, and re-layouts  25.8 us
    psum x1, blocking collectives, local(): lax.psum(lax.psum((jnp.sum(dshift * normed, axis=0), jnp.sum(dshift, axis...  22.5 us
  transfers between devices with their start and end apart: 7, of which 2 were waited for; matrix products, arithmetic and copies ran while one was open for 10% of the time, Pallas kernels for 0%

profile of v1, /device:TPU:1, one launch (start us, length us, event | category | flops | bytes accessed | tf_op | source)
XLA Modules:
  0.0 539.4 jit_solution(6138881993898332800)
XLA Ops:
  7.2 1.7 convert_bitcast_fusion
  9.7 1.2 bitcast_select_fusion
  10.9 8.8 %collective-permute-start = (bf16[1,128,320]{1,2,0:T(8,128)(2,1)S(1)}, bf16[1,128,320]{1,2,0:T(8,128)(2,1)S(1)}, u32[]{:S(2)}, u32[]{:S(2)}) collective-permute-start(bf16[1,128,320]{1,2,0:T(8,128)(2,1)S(1)} %get-tuple-element.48), channel_id=1, source_target_pairs={{16,0},{32,16},{48,32},{64,48},{80,64},{96,80},{112,96},{128,112},... | collective-permute-start | bytes 245768 | tf_op jit(solution)/shard_map/ppermute | solution.py:20
  19.7 1.9 collective-permute-start.1
  21.6 1.5 copy.30
  23.2 1.3 dynamic-slice.4
  27.5 1.1 fusion.6
  28.6 1.1 fusion.7
  34.9 8.4 %copy.29 = bf16[8,128,2880]{2,1,0:T(8,128)(2,1)} copy(bf16[8,128,2880]{1,2,0:T(8,128)(2,1)} %fusion.10) | data formatting | bytes 11796480 | tf_op jit(solution)/shard_map/concatenate | solution.py:48
  43.4 37.7 %all-gather.3.cloned.1.call-done = bf16[16,180,320]{2,1,0:T(8,128)(2,1)} async-done(((bf16[1,180,320]{2,1,0:T(8,128)(2,1)}), bf16[16,180,320]{2,1,0:T(8,128)(2,1)}) %all-gather.3.cloned.1.call-update) | async-done | bytes 1843216 | tf_op jit(solution)/shard_map/all_gather | solution.py:72
  81.1 2.8 reshape.78
  83.8 5.1 multiply_reduce_fusion.3
  89.1 71.5 %psum.63 = f32[32]{0:T(128)S(1)} all-reduce(f32[32]{0:T(128)S(1)} %reduce_sum.67), channel_id=1, replica_groups=mesh['tile'=32,'fsdp'=16] {'tile'}, use_global_device_ids=true, to_apply=%region_2.3 | all-reduce | flops 32 | bytes 256 | tf_op jit(solution)/shard_map/psum | solution.py:74
  161.4 62.7 %psum.64 = f32[32]{0:T(128)S(1)} all-reduce(f32[32]{0:T(128)S(1)} %reduce_sum.73), channel_id=1, replica_groups=mesh['tile'=32,'fsdp'=16] {'tile'}, use_global_device_ids=true, to_apply=%region_5.6 | all-reduce | flops 32 | bytes 256 | tf_op jit(solution)/shard_map/psum | solution.py:76
  224.3 3.5 multiply_reduce_fusion
  228.2 63.8 %all-reduce.4 = (f32[32]{0:T(128)S(1)}, f32[32]{0:T(128)S(1)}, f32[320]{0:T(512)S(1)}, f32[320]{0:T(512)S(1)}) all-reduce(f32[32]{0:T(128)S(1)} %reduce_sum.93, f32[32]{0:T(128)S(1)} %reduce_sum.90, f32[320]{0:T(512)S(1)} %get-tuple-element.32, f32[320]{0:T(512)S(1)} %get-tuple-element.35), channel_id=1, replica_groups=mesh['tile'=32,'fsdp'=16] {'tile'}, use_global_device_ids=true, to_apply=%region_11.12 | all-reduce | flops 704 | bytes 5632 | tf_op jit(solution)/shard_map/psum | solution.py:85
  293.3 7.4 %convolution_convert_fusion = bf16[2880,320]{1,0:T(8,128)(2,1)} fusion(bf16[1024,2880]{1,0:T(8,128)(2,1)} %bitcast.60, bf16[1024,320]{0,1:T(8,128)(2,1)S(1)} %multiply_convert_fusion), kind=kOutput, calls=%fused_computation | convolution fusion | flops 1888358400 | bytes 8396800 | tf_op jit(solution)/shard_map/dot_general | solution.py:108
  301.5 33.5 %fusion = bf16[192,320]{1,0:T(8,128)(2,1)S(1)} fusion(bf16[2880,320]{1,0:T(8,128)(2,1)} %convolution_convert_fusion), kind=kCustom, calls=%all-reduce-scatter | all-reduce-scatter fusion | flops 983041 | bytes 1968128
  335.1 2.7 collective-permute-start.4
  338.5 5.1 collective-permute-start.3
  343.5 5.3 collective-permute-start.2
  348.8 22.5 %all-reduce.5 = (f32[320]{0:T(512)S(1)}, f32[320]{0:T(512)S(1)}) all-reduce(f32[320]{0:T(512)S(1)} %get-tuple-element.38, f32[320]{0:T(512)S(1)} %get-tuple-element.39), channel_id=1, replica_groups=mesh['tile'=32,'fsdp'=16] {'fsdp'}, use_global_device_ids=true, to_apply=%region_16.17 | all-reduce | flops 640 | bytes 5120 | tf_op jit(solution)/shard_map/psum | solution.py:86
  371.9 2.2 reshape.73
  374.1 1.8 reverse_bitcast_fusion
  376.0 2.5 copy.34
  378.5 1.2 copy.38
  382.9 1.1 fusion.12
  384.0 1.1 fusion.13
  390.4 8.6 %copy.33 = bf16[8,128,2880]{2,1,0:T(8,128)(2,1)} copy(bf16[8,128,2880]{1,2,0:T(8,128)(2,1)} %fusion.16) | data formatting | bytes 11796480 | tf_op jit(solution)/shard_map/concatenate | solution.py:48
  400.6 5.0 fusion.4
  406.6 123.8 %all-reduce.8.cloned.1.call-done = bf16[180,320]{1,0:T(8,128)(2,1)} async-done(((bf16[180,320]{1,0:T(8,128)(2,1)}), bf16[180,320]{1,0:T(8,128)(2,1)}) %all-reduce.8.cloned.1.call-update) | async-done | bytes 115216 | tf_op jit(solution)/shard_map/psum | solution.py:107
  530.5 2.0 divide_subtract_fusion
  (78 shorter events, 23.8 us)
Async XLA Ops:
  7.2 14.4 %copy-start.3 = (bf16[1,1,8,128,320]{3,4,2,1,0:T(8,128)(2,1)S(1)}, bf16[1,1,8,128,320]{3,4,2,1,0:T(8,128)(2,1)}, u32[]{:S(2)}) copy-start(bf16[1,1,8,128,320]{3,4,2,1,0:T(8,128)(2,1)} %param.10) | copy-start | bytes 1966084
  7.2 73.9 %all-gather.3.cloned.1.call-start = ((), (), s32[]{:S(2)}) async-start(), calls=%async_computation.1 | async-start | bytes 2402304 | tf_op jit(solution)/shard_map/all_gather | solution.py:72
  8.9 521.5 %all-reduce.8.cloned.1.call-start = ((), (), s32[]{:S(2)}) async-start(), calls=%async_computation | async-start | bytes 282624 | tf_op jit(solution)/shard_map/psum | solution.py:107
  10.9 14.3 %collective-permute-start = (bf16[1,128,320]{1,2,0:T(8,128)(2,1)S(1)}, bf16[1,128,320]{1,2,0:T(8,128)(2,1)S(1)}, u32[]{:S(2)}, u32[]{:S(2)}) collective-permute-start(bf16[1,128,320]{1,2,0:T(8,128)(2,1)S(1)} %get-tuple-element.48), channel_id=1, source_target_pairs={{16,0},{32,16},{48,32},{64,48},{80,64},{96,80},{112,96},{128,112},... | collective-permute-start | bytes 245768 | tf_op jit(solution)/shard_map/ppermute | solution.py:20
  19.7 5.5 %collective-permute-start.1 = (bf16[1,128,320]{1,2,0:T(8,128)(2,1)S(1)}, bf16[1,128,320]{1,2,0:T(8,128)(2,1)S(1)}, u32[]{:S(2)}, u32[]{:S(2)}) collective-permute-start(bf16[1,128,320]{1,2,0:T(8,128)(2,1)S(1)} %get-tuple-element.49), channel_id=1, source_target_pairs={{0,16},{16,32},{32,48},{48,64},{64,80},{80,96},{96,112},{112,128},... | collective-permute-start | bytes 245768 | tf_op jit(solution)/shard_map/ppermute | solution.py:18
  83.8 140.5 %copy-start.6 = (f32[320]{0:T(512)S(1)}, f32[320]{0:T(512)}, u32[]{:S(2)}) copy-start(f32[320]{0:T(512)} %param.12) | copy-start | bytes 3844
  83.8 140.5 %copy-start.7 = (f32[320]{0:T(512)S(1)}, f32[320]{0:T(512)}, u32[]{:S(2)}) copy-start(f32[320]{0:T(512)} %param.13) | copy-start | bytes 3844
  300.7 71.2 %copy-start = (bf16[16,180,320]{2,1,0:T(8,128)(2,1)S(1)}, bf16[16,180,320]{2,1,0:T(8,128)(2,1)}, u32[]{:S(2)}) copy-start(bf16[16,180,320]{2,1,0:T(8,128)(2,1)} %all-gather.3.cloned.1.call-done) | copy-start | bytes 5529604
  335.1 63.9 %collective-permute-start.4 = (bf16[180,320]{1,0:T(8,128)(2,1)S(1)}, bf16[180,320]{1,0:T(8,128)(2,1)S(1)}, u32[]{:S(2)}, u32[]{:S(2)}) collective-permute-start(bf16[180,320]{1,0:T(8,128)(2,1)S(1)} %slice.98), channel_id=1, source_target_pairs={{0,1},{1,2},{2,3},{3,4},{4,5},{5,6},{6,7},{7,8},{8,9},{9,10},{10,1... | collective-permute-start | bytes 345608
  338.5 42.2 %collective-permute-start.3 = (bf16[1,128,320]{1,2,0:T(8,128)(2,1)}, bf16[1,128,320]{1,2,0:T(8,128)(2,1)S(1)}, u32[]{:S(2)}, u32[]{:S(2)}) collective-permute-start(bf16[1,128,320]{1,2,0:T(8,128)(2,1)} %constant_dynamic-slice_fusion.1), channel_id=1, source_target_pairs={{0,16},{16,32},{32,48},{48,64},{64,80},{80,96},{96,112},{112,128},... | collective-permute-start | bytes 245768 | tf_op jit(solution)/shard_map/ppermute | solution.py:18
  343.5 37.1 %collective-permute-start.2 = (bf16[1,128,320]{1,2,0:T(8,128)(2,1)}, bf16[1,128,320]{1,2,0:T(8,128)(2,1)S(1)}, u32[]{:S(2)}, u32[]{:S(2)}) collective-permute-start(bf16[1,128,320]{1,2,0:T(8,128)(2,1)} %slice_bitcast_fusion), channel_id=1, source_target_pairs={{16,0},{32,16},{48,32},{64,48},{80,64},{96,80},{112,96},{128,112},... | collective-permute-start | bytes 245768 | tf_op jit(solution)/shard_map/ppermute | solution.py:20
  390.4 10.2 %copy-start.1 = (bf16[9,320,320]{2,1,0:T(8,128)(2,1)S(1)}, bf16[9,320,320]{2,1,0:T(8,128)(2,1)}, u32[]{:S(2)}) copy-start(bf16[9,320,320]{2,1,0:T(8,128)(2,1)} %copy.34) | copy-start | bytes 5529604
  405.5 125.0 %copy-start.2 = (f32[180,320]{1,0:T(8,128)S(1)}, f32[180,320]{1,0:T(8,128)}, u32[]{:S(2)}) copy-start(f32[180,320]{1,0:T(8,128)} %param.11) | copy-start | bytes 691204
  405.5 124.9 %copy-start.4 = (f32[180,320]{1,0:T(8,128)S(1)}, f32[180,320]{1,0:T(8,128)}, u32[]{:S(2)}) copy-start(f32[180,320]{1,0:T(8,128)} %param.14) | copy-start | bytes 691204
  405.6 124.9 %copy-start.5 = (f32[180,320]{1,0:T(8,128)S(1)}, f32[180,320]{1,0:T(8,128)}, u32[]{:S(2)}) copy-start(f32[180,320]{1,0:T(8,128)} %param.15) | copy-start | bytes 691204
Sparse Core Ops, SparseCore 0:
  10.7 70.3 all-gather.2
  400.7 129.7 all-reduce.7
